TPU v7x, 32 devices: a whole 2x2x4 slice. The times are simulated.
32 devices in a mesh: seq: 4 (over x, core), shard: 8 (over z, y).
Axes of the slice: x: 2, y: 2, z: 4, core: 2. Of those that a mesh axis runs over, the one named last changes fastest.
Arguments:
- inputs: bfloat16 [8, 3072, 768], P('shard', 'seq'), may hold values from -6 to 6
- teacher: bfloat16 [8, 3072, 768], P('shard', 'seq'), may hold values from -6 to 6
- seq_lengths: int32 [8, 3], P('shard'), may hold values from 0 to 3072, as said below
- w_qkv: bfloat16 [768, 2304], P('shard'), may hold values from -0.21875 to 0.21875
- q_bias: bfloat16 [768], P('shard'), may hold values from -4 to 4
- v_bias: bfloat16 [768], P('shard'), may hold values from -0.75 to 0.75
- w_out: bfloat16 [768, 768], P('shard'), may hold values from -3.5 to 3.5
- out_bias: bfloat16 [768], P('shard'), may hold values from -4 to 4
- attn_gain: bfloat16 [768], P('shard'), may hold values from 0.5 to 1.5
- attn_shift: bfloat16 [768], P('shard'), may hold values from -4 to 4
- w_up: bfloat16 [768, 3072], P('shard'), may hold values from -0.21875 to 0.21875
- up_bias: bfloat16 [3072], P('shard'), may hold values from -4 to 4
- w_down: bfloat16 [3072, 768], P('shard'), may hold values from -0.109375 to 0.109375
- down_bias: bfloat16 [768], P('shard'), may hold values from -4 to 4
- ffn_gain: bfloat16 [768], P('shard'), may hold values from 0.5 to 1.5
- ffn_shift: bfloat16 [768], P('shard'), may hold values from -4 to 4
Outputs:
- layer_out: bfloat16 [8, 3072, 768], P('shard', 'seq')
- input_grad: bfloat16 [8, 3072, 768], P('shard', 'seq')
- grad_qkv: float32 [768, 2304], P('shard')
- grad_q_bias: float32 [768], P('shard')
- grad_v_bias: float32 [768], P('shard')
- grad_out: float32 [768, 768], P('shard')
- grad_out_bias: float32 [768], P('shard')
- grad_attn_gain: float32 [768], P('shard')
- grad_attn_shift: float32 [768], P('shard')
- grad_up: float32 [768, 3072], P('shard')
- grad_up_bias: float32 [3072], P('shard')
- grad_down: float32 [3072, 768], P('shard')
- grad_down_bias: float32 [768], P('shard')
- grad_ffn_gain: float32 [768], P('shard')
- grad_ffn_shift: float32 [768], P('shard')
Inputs may be any that keep to these rules, and one draw needn't show every extreme that they name: `seq_lengths`: each row lists the lengths of the sequences packed from the start of one group's 3072 slots; the used slots come first and each holds 1024 tokens or more, the unused ones are 0; a row sums to at most 3072; some row holds a single sequence of 3072 tokens; the slots after a row's sum are padding.
All inputs are finite; a program needn't handle non-finite values.
Results may differ from a plain program's by a relative error of at most 0.01.
Values may be sent and summed in bfloat16 or wider, within the bound.
A program may use at most 128 MiB of HBM per device.

v0:
```python
import jax
import jax.numpy as jnp
from jax import lax
from jax.sharding import PartitionSpec as P

HEADS = 12
HD = 64
epsilon = 1e-12
neg_large = -1e30


def layer_norm(value, gain, shift):
    mean_val = jnp.mean(value, axis=-1, keepdims=True)
    centred = value - mean_val
    variance = jnp.mean(centred * centred, axis=-1, keepdims=True)
    return centred * lax.rsqrt(variance + epsilon) * gain + shift


def exact_gelu(value):
    return jax.nn.gelu(value, approximate=False)


def contract_rows(left, right):
    return lax.dot_general(
        left, right, (((0,), (0,)), ((), ())), preferred_element_type=jnp.float32
    )


def contract_cols(left, right):
    return lax.dot_general(
        left, right, (((1,), (1,)), ((), ())), preferred_element_type=jnp.float32
    )


def on_device(
    inputs,
    teacher,
    seq_lengths,
    w_qkv,
    q_bias,
    v_bias,
    w_out,
    out_bias,
    attn_gain,
    attn_shift,
    w_up,
    up_bias,
    w_down,
    down_bias,
    ffn_gain,
    ffn_shift,
):
    tok_rows = inputs.shape[1]
    model_width = inputs.shape[2]
    seq_parts = lax.axis_size("seq")
    group_rows = tok_rows * seq_parts
    heads_dev = HEADS // seq_parts
    head_cols = heads_dev * HD
    block_rows = min(512, group_rows)
    nblocks = group_rows // block_rows
    score_scale = HD ** (-0.5)
    tokens = inputs[0]
    targets = teacher[0].astype(jnp.float32)
    seq_ends = jnp.cumsum(seq_lengths[0])
    all_pos = lax.iota(jnp.int32, group_rows)
    all_seg = jnp.sum((all_pos[:, None] >= seq_ends[None, :]).astype(jnp.int32), axis=1)
    own_seg = lax.dynamic_slice_in_dim(all_seg, lax.axis_index("seq") * tok_rows, tok_rows)
    live_rows = (own_seg < seq_lengths.shape[1]).astype(jnp.float32)
    live_total = lax.psum(seq_ends[-1].astype(jnp.float32), "shard")
    full_qkv, full_q_bias, full_v_bias, full_out, full_out_bias, full_attn_gain, full_attn_shift = (
        lax.all_gather(w_qkv, "shard", axis=0, tiled=True),
        lax.all_gather(q_bias, "shard", axis=0, tiled=True),
        lax.all_gather(v_bias, "shard", axis=0, tiled=True),
        lax.all_gather(w_out, "shard", axis=0, tiled=True),
        lax.all_gather(out_bias, "shard", axis=0, tiled=True),
        lax.all_gather(attn_gain, "shard", axis=0, tiled=True),
        lax.all_gather(attn_shift, "shard", axis=0, tiled=True),
    )
    bias_row = jnp.concatenate([full_q_bias, jnp.zeros_like(full_q_bias), full_v_bias]).astype(
        jnp.float32
    )
    projected = jnp.dot(tokens, full_qkv, preferred_element_type=jnp.float32) + bias_row
    projected = projected.astype(jnp.bfloat16).reshape(tok_rows, 3, seq_parts, head_cols)
    by_heads = lax.all_to_all(projected, "seq", split_axis=2, concat_axis=0, tiled=True)
    queries = by_heads[:, 0, 0]
    keys = by_heads[:, 1, 0]
    values = by_heads[:, 2, 0]

    def block_scores(q_blk, k_head, row_start):
        seg_blk = lax.dynamic_slice_in_dim(all_seg, row_start, block_rows)
        raw = contract_cols(q_blk, k_head) * score_scale
        return jnp.where(seg_blk[:, None] == all_seg[None, :], raw, neg_large)

    def attend(state_in, flat_idx):
        head_idx = flat_idx // nblocks
        row_start = flat_idx % nblocks * block_rows
        q_blk = lax.dynamic_slice(queries, (row_start, head_idx * HD), (block_rows, HD))
        k_head = lax.dynamic_slice_in_dim(keys, head_idx * HD, HD, 1)
        v_head = lax.dynamic_slice_in_dim(values, head_idx * HD, HD, 1)
        scores = block_scores(q_blk, k_head, row_start)
        row_max = jnp.max(scores, axis=1, keepdims=True)
        exp_scores = jnp.exp(scores - row_max)
        row_sum = jnp.sum(exp_scores, axis=1, keepdims=True)
        probs_low = (exp_scores / row_sum).astype(jnp.bfloat16)
        ctx_blk = jnp.dot(probs_low, v_head, preferred_element_type=jnp.float32)
        return (state_in, (ctx_blk.astype(jnp.bfloat16), (row_max + jnp.log(row_sum))[:, 0]))

    flat_ids = jnp.arange(heads_dev * nblocks, dtype=jnp.int32)
    _, (ctx_blocks, lse_blocks) = lax.scan(attend, 0, flat_ids)
    context = jnp.transpose(ctx_blocks.reshape(heads_dev, group_rows, HD), (1, 0, 2)).reshape(
        group_rows, head_cols
    )
    lse_all = lse_blocks.reshape(heads_dev, group_rows)
    merged = lax.all_to_all(
        context.reshape(group_rows, 1, head_cols), "seq", split_axis=0, concat_axis=1, tiled=True
    ).reshape(tok_rows, model_width)
    branch = jnp.dot(merged, full_out, preferred_element_type=jnp.float32) + full_out_bias.astype(
        jnp.float32
    )
    resid_one = tokens.astype(jnp.float32) + branch
    normed, norm_one_back = jax.vjp(
        layer_norm,
        resid_one,
        full_attn_gain.astype(jnp.float32),
        full_attn_shift.astype(jnp.float32),
    )
    full_up, full_up_bias, full_down, full_down_bias, full_ffn_gain, full_ffn_shift = (
        lax.all_gather(w_up, "shard", axis=0, tiled=True),
        lax.all_gather(up_bias, "shard", axis=0, tiled=True),
        lax.all_gather(w_down, "shard", axis=0, tiled=True),
        lax.all_gather(down_bias, "shard", axis=0, tiled=True),
        lax.all_gather(ffn_gain, "shard", axis=0, tiled=True),
        lax.all_gather(ffn_shift, "shard", axis=0, tiled=True),
    )
    normed_low = normed.astype(jnp.bfloat16)
    pre_act = jnp.dot(
        normed_low, full_up, preferred_element_type=jnp.float32
    ) + full_up_bias.astype(jnp.float32)
    activated, gelu_back = jax.vjp(exact_gelu, pre_act)
    act_low = activated.astype(jnp.bfloat16)
    ffn_out = jnp.dot(
        act_low, full_down, preferred_element_type=jnp.float32
    ) + full_down_bias.astype(jnp.float32)
    resid_two = normed + ffn_out
    result, norm_two_back = jax.vjp(
        layer_norm, resid_two, full_ffn_gain.astype(jnp.float32), full_ffn_shift.astype(jnp.float32)
    )
    loss_scale = float(group_rows * lax.axis_size("shard"))
    grad_result = (result - targets) * live_rows[:, None] * (loss_scale / live_total)
    back_qkv, back_out = (
        lax.all_gather(w_qkv, "shard", axis=0, tiled=True),
        lax.all_gather(w_out, "shard", axis=0, tiled=True),
    )
    back_up, back_down = (
        lax.all_gather(w_up, "shard", axis=0, tiled=True),
        lax.all_gather(w_down, "shard", axis=0, tiled=True),
    )
    grad_resid_two, grad_ffn_gain, grad_ffn_shift = norm_two_back(grad_result)
    grad_ffn_low = grad_resid_two.astype(jnp.bfloat16)
    grad_down = contract_rows(act_low, grad_ffn_low)
    grad_down_bias = jnp.sum(grad_ffn_low, axis=0, dtype=jnp.float32)
    grad_act = contract_cols(grad_ffn_low, back_down)
    (grad_pre_full,) = gelu_back(grad_act)
    grad_pre = grad_pre_full.astype(jnp.bfloat16)
    grad_up = contract_rows(normed_low, grad_pre)
    grad_up_bias = jnp.sum(grad_pre, axis=0, dtype=jnp.float32)
    grad_normed = contract_cols(grad_pre, back_up) + grad_resid_two
    grad_resid_one, grad_attn_gain, grad_attn_shift = norm_one_back(grad_normed)
    grad_branch = grad_resid_one.astype(jnp.bfloat16)
    grad_out = contract_rows(merged, grad_branch)
    grad_out_bias = jnp.sum(grad_branch, axis=0, dtype=jnp.float32)
    grad_merged = contract_cols(grad_branch, back_out).astype(jnp.bfloat16)
    grad_context = lax.all_to_all(
        grad_merged.reshape(tok_rows, seq_parts, head_cols),
        "seq",
        split_axis=1,
        concat_axis=0,
        tiled=True,
    ).reshape(group_rows, head_cols)

    def head_back(state_in, head_idx):
        k_head = lax.dynamic_slice_in_dim(keys, head_idx * HD, HD, 1)
        v_head = lax.dynamic_slice_in_dim(values, head_idx * HD, HD, 1)
        lse_head = lax.dynamic_index_in_dim(lse_all, head_idx, 0, keepdims=False)

        def block_back(sums, blk_idx):
            grad_keys, grad_values = sums
            row_start = blk_idx * block_rows
            q_blk = lax.dynamic_slice(queries, (row_start, head_idx * HD), (block_rows, HD))
            dctx_blk = lax.dynamic_slice(grad_context, (row_start, head_idx * HD), (block_rows, HD))
            lse_blk = lax.dynamic_slice_in_dim(lse_head, row_start, block_rows)
            scores = block_scores(q_blk, k_head, row_start)
            probs = jnp.exp(scores - lse_blk[:, None])
            probs_low = probs.astype(jnp.bfloat16)
            grad_probs = contract_cols(dctx_blk, v_head)
            delta = jnp.sum(grad_probs * probs, axis=1, keepdims=True)
            grad_scores = (probs * (grad_probs - delta)).astype(jnp.bfloat16)
            grad_values = grad_values + contract_rows(probs_low, dctx_blk)
            grad_keys = grad_keys + contract_rows(grad_scores, q_blk) * score_scale
            dq_blk = jnp.dot(grad_scores, k_head, preferred_element_type=jnp.float32) * score_scale
            return ((grad_keys, grad_values), dq_blk)

        zero_head = jnp.zeros((group_rows, HD), jnp.float32)
        (grad_keys, grad_values), dq_blocks = lax.scan(
            block_back, (zero_head, zero_head), jnp.arange(nblocks, dtype=jnp.int32)
        )
        return (state_in, (dq_blocks.reshape(group_rows, HD), grad_keys, grad_values))

    _, (grad_q_heads, grad_k_heads, grad_v_heads) = lax.scan(
        head_back, 0, jnp.arange(heads_dev, dtype=jnp.int32)
    )

    def side_by_side(per_head):
        return jnp.transpose(per_head, (1, 0, 2)).reshape(group_rows, head_cols)

    stacked = jnp.stack(
        [side_by_side(grad_q_heads), side_by_side(grad_k_heads), side_by_side(grad_v_heads)], axis=1
    ).astype(jnp.bfloat16)
    grad_proj = lax.all_to_all(
        stacked[:, :, None, :], "seq", split_axis=0, concat_axis=2, tiled=True
    ).reshape(tok_rows, 3 * model_width)
    grad_qkv = contract_rows(tokens, grad_proj)
    grad_q_bias = jnp.sum(grad_proj[:, :model_width], axis=0, dtype=jnp.float32)
    grad_v_bias = jnp.sum(grad_proj[:, 2 * model_width :], axis=0, dtype=jnp.float32)
    grad_inputs = grad_resid_one + contract_cols(grad_proj, back_qkv)
    owned = (
        lax.psum_scatter(grad_qkv, "shard", scatter_dimension=0, tiled=True),
        lax.psum_scatter(grad_q_bias, "shard", scatter_dimension=0, tiled=True),
        lax.psum_scatter(grad_v_bias, "shard", scatter_dimension=0, tiled=True),
        lax.psum_scatter(grad_out, "shard", scatter_dimension=0, tiled=True),
        lax.psum_scatter(grad_out_bias, "shard", scatter_dimension=0, tiled=True),
        lax.psum_scatter(grad_attn_gain, "shard", scatter_dimension=0, tiled=True),
        lax.psum_scatter(grad_attn_shift, "shard", scatter_dimension=0, tiled=True),
        lax.psum_scatter(grad_up, "shard", scatter_dimension=0, tiled=True),
        lax.psum_scatter(grad_up_bias, "shard", scatter_dimension=0, tiled=True),
        lax.psum_scatter(grad_down, "shard", scatter_dimension=0, tiled=True),
        lax.psum_scatter(grad_down_bias, "shard", scatter_dimension=0, tiled=True),
        lax.psum_scatter(grad_ffn_gain, "shard", scatter_dimension=0, tiled=True),
        lax.psum_scatter(grad_ffn_shift, "shard", scatter_dimension=0, tiled=True),
    )
    summed = (
        lax.psum(owned[0].astype(jnp.bfloat16), "seq").astype(jnp.float32),
        lax.psum(owned[1].astype(jnp.bfloat16), "seq").astype(jnp.float32),
        lax.psum(owned[2].astype(jnp.bfloat16), "seq").astype(jnp.float32),
        lax.psum(owned[3].astype(jnp.bfloat16), "seq").astype(jnp.float32),
        lax.psum(owned[4].astype(jnp.bfloat16), "seq").astype(jnp.float32),
        lax.psum(owned[5].astype(jnp.bfloat16), "seq").astype(jnp.float32),
        lax.psum(owned[6].astype(jnp.bfloat16), "seq").astype(jnp.float32),
        lax.psum(owned[7].astype(jnp.bfloat16), "seq").astype(jnp.float32),
        lax.psum(owned[8].astype(jnp.bfloat16), "seq").astype(jnp.float32),
        lax.psum(owned[9].astype(jnp.bfloat16), "seq").astype(jnp.float32),
        lax.psum(owned[10].astype(jnp.bfloat16), "seq").astype(jnp.float32),
        lax.psum(owned[11].astype(jnp.bfloat16), "seq").astype(jnp.float32),
        lax.psum(owned[12].astype(jnp.bfloat16), "seq").astype(jnp.float32),
    )
    return (
        result.astype(jnp.bfloat16)[None],
        grad_inputs.astype(jnp.bfloat16)[None],
        summed[0],
        summed[1],
        summed[2],
        summed[3],
        summed[4],
        summed[5],
        summed[6],
        summed[7],
        summed[8],
        summed[9],
        summed[10],
        summed[11],
        summed[12],
    )


def solution(mesh):
    in_specs = (
        P("shard", "seq", None),
        P("shard", "seq", None),
        P("shard", None),
        P("shard", None),
        P("shard"),
        P("shard"),
        P("shard", None),
        P("shard"),
        P("shard"),
        P("shard"),
        P("shard", None),
        P("shard"),
        P("shard", None),
        P("shard"),
        P("shard"),
        P("shard"),
    )
    out_specs = (
        P("shard", "seq", None),
        P("shard", "seq", None),
        P("shard", None),
        P("shard"),
        P("shard"),
        P("shard", None),
        P("shard"),
        P("shard"),
        P("shard"),
        P("shard", None),
        P("shard"),
        P("shard", None),
        P("shard"),
        P("shard"),
        P("shard"),
    )
    return jax.shard_map(
        on_device, mesh=mesh, in_specs=in_specs, out_specs=out_specs, check_vma=False
    )
```

profile of v0, /device:TPU:0, one launch (start us, length us, event | category | flops | bytes accessed | tf_op | source)
XLA Modules:
  0.0 1513.0 jit_solution(15992502380309811443)
XLA Ops:
  18.1 40.2 %all-reduce.18 = (bf16[768]{0:T(1024)(128)(2,1)S(1)}, bf16[768]{0:T(1024)(128)(2,1)S(1)}, bf16[768]{0:T(1024)(128)(2,1)}, bf16[768]{0:T(1024)(128)(2,1)}, bf16[7...) all-reduce(bf16[768]{0:T(1024)(128)(2,1)S(1)} %dynamic-update-slice, ...), channel_id=1, replica_groups=mesh['seq'=4,'shard'=8] {'shard'}, use_global_device_ids=true, to_apply=%add.1 | all-reduce | flops 6144 | bytes 24576
  58.3 20.2 %all-gather.6.cloned.1.call-done = bf16[768,2304]{1,0:T(8,128)(2,1)} async-done(((bf16[96,2304]{1,0:T(8,128)(2,1)}), bf16[768,2304]{1,0:T(8,128)(2,1)}) %all-gather.6.cloned.1.call-update) | async-done | bytes 3538960 | tf_op jit(solution)/shard_map/all_gather | solution.py:71
  98.2 39.1 %all-to-all-done = bf16[768,3,4,192]{0,3,1,2:T(8,128)(2,1)S(1)} async-done(((bf16[768,3,4,192]{0,3,1,2:T(8,128)(2,1)}), bf16[768,3,4,192]{0,3,1,2:T(8,128)(2,1)S(1)}, u32[]{:S(2)}, u32[]{:S(2)}) %all-to-all-start) | async-done | bytes 3538976 | tf_op jit(solution)/shard_map/all_to_all | solution.py:84
  142.8 189.0 %while.45 = (s32[]{:T(128)}, bf16[18,512,64]{1,2,0:T(8,128)(2,1)S(1)}, f32[18,512]{1,0:T(8,128)}, s32[18]{0:T(128)S(1)}, s32[3072]{0:T(1024)S(1)}, /*index=5*/bf...) while((s32[]{:T(128)}, ...), condition=%wide.region_5.6_spmd, body=%wide.region_2.0_spmd.sunk | while | flops 416841216 | bytes 20684696 | solution.py:109
  345.3 20.4 %psum.98 = f32[]{:T(128)} all-reduce(f32[]{:T(128)} %bitcast.27), channel_id=1, replica_groups=mesh['seq'=4,'shard'=8] {'shard'}, use_global_device_ids=true, to_apply=%region_10.11 | all-reduce | flops 1 | bytes 8 | tf_op jit(solution)/shard_map/psum | solution.py:69
  367.7 25.9 %all-gather = bf16[8,1,384]{2,1,0:T(2,128)(2,1)S(1)} all-gather(bf16[1,1,384]{2,1,0:T(2,128)(2,1)S(1)} %reshape.280), channel_id=1, replica_groups=mesh['seq'=4,'shard'=8] {'shard'}, dimensions={0}, use_global_device_ids=true | all-gather | bytes 6912 | tf_op jit(solution)/shard_map/all_gather | solution.py:129
  416.9 28.7 %multiply_convert_fusion.1 = (bf16[768,3072]{1,0:T(8,128)(2,1)}, f32[768,3072]{1,0:T(8,128)}, f32[768,3072]{1,0:T(8,128)}) fusion(f32[3072]{0:T(1024)} %bitcast.163, bf16[768,3072]{1,0:T(8,128)(2,1)} %all-gather.10.cloned.1.call-done, f32[768,768]{0,1:T(8,128)S(1)} %get-tuple-element.713, f32[768]{0:T(1024)} %convert_element_type.205, ...), kind=kOutput, calls=%fused_computation.39 | convolution fusion | flops 3782541312 | bytes 30695424 | tf_op jit(solution)/shard_map/dot_general | solution.py:136
  445.6 7.7 fusion.47
  460.0 13.5 convert_reduce_fusion
  473.6 7.6 multiply_reduce_fusion.2
  493.7 11.8 all-to-all-done.2
  507.1 362.0 %while.47 = (s32[]{:T(128)}, bf16[3,3072,64]{1,2,0:T(8,128)(2,1)}, bf16[3,3072,64]{1,2,0:T(8,128)(2,1)}, bf16[3,3072,64]{1,2,0:T(8,128)(2,1)}, s32[3]{0:T(128)S(...) while((s32[]{:T(128)}, bf16[3,3072,64]{1,2,0:T(8,128)(2,1)}, ...), condition=%wide.region_19.20_spmd, body=%wide.region_15.19_spmd.sunk | while | flops 1023376896 | bytes 123100080 | solution.py:209
  516.5 109.1 %while.48 = (s32[]{:T(128)}, f32[3072,64]{0,1:T(8,128)}, f32[3072,64]{0,1:T(8,128)}, bf16[6,512,64]{1,2,0:T(8,128)(2,1)S(1)}, s32[6]{0:T(128)}, /*index=5*/s32[3...) while((s32[]{:T(128)}, f32[3072,64]{0,1:T(8,128)}, ...), condition=%wide.region_18.18_spmd.clone, body=%wide.region_16.17_spmd.clone.sunk | while | flops 1023376896 | bytes 109607288 | solution.py:204
  637.3 108.8 %while.48 = (s32[]{:T(128)}, f32[3072,64]{0,1:T(8,128)}, f32[3072,64]{0,1:T(8,128)}, bf16[6,512,64]{1,2,0:T(8,128)(2,1)S(1)}, s32[6]{0:T(128)}, /*index=5*/s32[3...) while((s32[]{:T(128)}, f32[3072,64]{0,1:T(8,128)}, ...), condition=%wide.region_18.18_spmd.clone, body=%wide.region_16.17_spmd.clone.sunk | while | flops 1023376896 | bytes 109607288 | solution.py:204
  757.9 108.8 %while.48 = (s32[]{:T(128)}, f32[3072,64]{0,1:T(8,128)}, f32[3072,64]{0,1:T(8,128)}, bf16[6,512,64]{1,2,0:T(8,128)(2,1)S(1)}, s32[6]{0:T(128)}, /*index=5*/s32[3...) while((s32[]{:T(128)}, f32[3072,64]{0,1:T(8,128)}, ...), condition=%wide.region_18.18_spmd.clone, body=%wide.region_16.17_spmd.clone.sunk | while | flops 1023376896 | bytes 109607288 | solution.py:204
  878.3 77.3 %all_to_all.63 = bf16[3072,3,1,192]{3,1,2,0:T(4,128)(2,1)} all-to-all(bf16[3072,3,1,192]{3,1,2,0:T(4,128)(2,1)} %copy.198), channel_id=1, replica_groups=mesh['seq'=4,'shard'=8] {'seq'}, dimensions={0} | all-to-all | bytes 7077888 | tf_op jit(solution)/shard_map/all_to_all | solution.py:219
  955.6 10.5 copy.208
  973.4 8.1 copy.209
  983.1 9.7 fusion.37
  994.1 8.8 fusion.49
  1007.5 99.3 %reduce-scatter.13.cloned.1.call-done = f32[96,2304]{1,0:T(8,128)} async-done(((f32[768,2304]{1,0:T(8,128)}), f32[96,2304]{1,0:T(8,128)}) %reduce-scatter.13.cloned.1.call-update) | async-done | bytes 884752
  1109.0 164.3 %reduce-scatter.9.cloned.1.call-done = f32[96,3072]{1,0:T(8,128)} async-done(((f32[768,3072]{1,0:T(8,128)}), f32[96,3072]{1,0:T(8,128)}) %reduce-scatter.9.cloned.1.call-update) | async-done | bytes 1179664 | tf_op jit(solution)/shard_map/reduce_scatter | solution.py:234
  1275.5 164.5 %reduce-scatter.11.cloned.1.call-done = f32[384,768]{1,0:T(8,128)} async-done(((f32[3072,768]{1,0:T(8,128)}), f32[384,768]{1,0:T(8,128)}) %reduce-scatter.11.cloned.1.call-update) | async-done | bytes 1179664 | tf_op jit(solution)/shard_map/reduce_scatter | solution.py:236
  1451.6 36.1 %all-reduce.17 = (bf16[768]{0:T(1024)(128)(2,1)S(1)}, bf16[768]{0:T(1024)(128)(2,1)S(1)}, bf16[768]{0:T(1024)(128)(2,1)S(1)}, bf16[768]{0:T(1024)(128)(2,1)S(1)}...) all-reduce(f32[768]{0:T(1024)S(1)} %get-tuple-element.594, ...), channel_id=3, replica_groups=mesh['seq'=4,'shard'=8] {'shard'}, use_global_device_ids=true, to_apply=%region_23.24.clone | all-reduce | flops 9216 | bytes 55296
  (723 shorter events, 643.8 us)
Async XLA Ops:
  7.2 71.4 %all-gather.6.cloned.1.call-start = ((), (), s32[]{:S(2)}) async-start(), calls=%async_computation.8 | async-start | bytes 3981312 | tf_op jit(solution)/shard_map/all_gather | solution.py:71
  7.9 404.4 %all-gather.8.cloned.1.call-start = ((), (), s32[]{:S(2)}) async-start(), calls=%async_computation.9 | async-start | bytes 1327104 | tf_op jit(solution)/shard_map/all_gather | solution.py:74
  8.7 408.2 %all-gather.10.cloned.1.call-start = ((), (), s32[]{:S(2)}) async-start(), calls=%async_computation.10 | async-start | bytes 5308416 | tf_op jit(solution)/shard_map/all_gather | solution.py:128
  92.3 45.0 %all-to-all-start = ((bf16[768,3,4,192]{0,3,1,2:T(8,128)(2,1)}), bf16[768,3,4,192]{0,3,1,2:T(8,128)(2,1)S(1)}, u32[]{:S(2)}, u32[]{:S(2)}) async-start(bf16[768,3,4,192]{0,3,1,2:T(8,128)(2,1)} %copy.178), calls=%async_computation | async-start | bytes 7077888 | tf_op jit(solution)/shard_map/all_to_all | solution.py:84
  96.2 349.5 %all-gather.12.cloned.1.call-start = ((), (), s32[]{:S(2)}) async-start(), calls=%async_computation.11 | async-start | bytes 5308416 | tf_op jit(solution)/shard_map/all_gather | solution.py:130
  336.7 28.9 %copy-start.16 = (bf16[1,768,768]{2,1,0:T(8,128)(2,1)S(1)}, bf16[1,768,768]{2,1,0:T(8,128)(2,1)}, u32[]{:S(2)}) copy-start(bf16[1,768,768]{2,1,0:T(8,128)(2,1)} %param.22) | copy-start | bytes 3538948
  339.6 28.1 %copy-start.44 = (bf16[384]{0:T(512)(128)(2,1)S(1)}, bf16[384]{0:T(512)(128)(2,1)}, u32[]{:S(2)}) copy-start(bf16[384]{0:T(512)(128)(2,1)} %param.33) | copy-start | bytes 2308
  339.6 54.6 %copy-start.43 = (bf16[768]{0:T(1024)(128)(2,1)S(1)}, bf16[768]{0:T(1024)(128)(2,1)}, u32[]{:S(2)}) copy-start(bf16[768]{0:T(1024)(128)(2,1)} %get-tuple-element.669) | copy-start | bytes 4612
  339.6 54.7 %copy-start.42 = (bf16[768]{0:T(1024)(128)(2,1)S(1)}, bf16[768]{0:T(1024)(128)(2,1)}, u32[]{:S(2)}) copy-start(bf16[768]{0:T(1024)(128)(2,1)} %get-tuple-element.670) | copy-start | bytes 4612
  339.6 55.2 %copy-start.41 = (bf16[768]{0:T(1024)(128)(2,1)S(1)}, bf16[768]{0:T(1024)(128)(2,1)}, u32[]{:S(2)}) copy-start(bf16[768]{0:T(1024)(128)(2,1)} %get-tuple-element.671) | copy-start | bytes 4612
  339.6 55.8 %copy-start.15 = (bf16[1,768,768]{2,1,0:T(8,128)(2,1)S(1)}, bf16[1,768,768]{2,1,0:T(8,128)(2,1)}, u32[]{:S(2)}) copy-start(bf16[1,768,768]{2,1,0:T(8,128)(2,1)} %param.23) | copy-start | bytes 3538948
  339.6 60.3 %all-to-all-start.1 = ((bf16[4,2,73728]{2,1,0:T(2,128)(2,1)}), bf16[4,2,73728]{2,1,0:T(2,128)(2,1)}, u32[]{:S(2)}, u32[]{:S(2)}) async-start(bf16[4,2,73728]{2,1,0:T(2,128)(2,1)} %reshape.310), calls=%async_computation.1 | async-start | bytes 2359296 | tf_op jit(solution)/shard_map/all_to_all | solution.py:114
  365.7 31.6 %copy-start.40 = (bf16[768]{0:T(1024)(128)(2,1)S(1)}, bf16[768]{0:T(1024)(128)(2,1)}, u32[]{:S(2)}) copy-start(bf16[768]{0:T(1024)(128)(2,1)} %get-tuple-element.673) | copy-start | bytes 4612
  365.7 32.2 %copy-start.39 = (bf16[768]{0:T(1024)(128)(2,1)S(1)}, bf16[768]{0:T(1024)(128)(2,1)}, u32[]{:S(2)}) copy-start(bf16[768]{0:T(1024)(128)(2,1)} %get-tuple-element.674) | copy-start | bytes 4612
  415.2 66.0 %copy-start.10 = (f32[768,768]{0,1:T(8,128)}, f32[768,768]{0,1:T(8,128)S(1)}, u32[]{:S(2)}) copy-start(f32[768,768]{0,1:T(8,128)S(1)} %get-tuple-element.713) | copy-start | bytes 7077892
  415.2 66.0 %copy-start.22 = (f32[768]{0:T(1024)}, f32[768]{0:T(1024)S(1)}, u32[]{:S(2)}) copy-start(f32[768]{0:T(1024)S(1)} %broadcast_multiply_fusion.1) | copy-start | bytes 9220
  486.0 19.4 %all-to-all-start.2 = ((bf16[768,4,192]{0,2,1:T(8,128)(2,1)}), bf16[768,4,192]{0,2,1:T(8,128)(2,1)S(1)}, u32[]{:S(2)}, u32[]{:S(2)}) async-start(bf16[768,4,192]{0,2,1:T(8,128)(2,1)} %bitcast.160), calls=%async_computation.2 | async-start | bytes 2359296 | tf_op jit(solution)/shard_map/all_to_all | solution.py:173
  489.6 516.2 %reduce-scatter.7.cloned.1.call-start = ((), (), s32[]{:S(2)}) async-start(), calls=%async_computation.12 | async-start | bytes 2654208 | tf_op jit(solution)/shard_map/reduce_scatter | solution.py:230
  493.6 613.2 %reduce-scatter.13.cloned.1.call-start = ((), (), s32[]{:S(2)}) async-start(), calls=%async_computation.15 | async-start | bytes 7962624
  981.5 291.9 %reduce-scatter.9.cloned.1.call-start = ((), (), s32[]{:S(2)}) async-start(), calls=%async_computation.13 | async-start | bytes 10616832 | tf_op jit(solution)/shard_map/reduce_scatter | solution.py:234
  992.9 447.1 %reduce-scatter.11.cloned.1.call-start = ((), (), s32[]{:S(2)}) async-start(), calls=%async_computation.14 | async-start | bytes 10616832 | tf_op jit(solution)/shard_map/reduce_scatter | solution.py:236
  1002.9 496.0 %all-reduce.23.cloned.1.call-start = ((), (), s32[]{:S(2)}) async-start(), calls=%async_computation.16 | async-start | bytes 3833856 | tf_op jit(solution)/shard_map/psum | solution.py:242
  1109.0 333.2 %copy-start.8 = (bf16[768,3,4,1,192]{0,4,2,1,3:T(8,128)(2,1)S(1)}, bf16[768,3,4,1,192]{0,4,2,1,3:T(8,128)(2,1)}, u32[]{:S(2)}) copy-start(bf16[768,3,4,1,192]{0,4,2,1,3:T(8,128)(2,1)} %copy-done.7) | copy-start | bytes 10616836
  1109.0 333.2 %copy-start.32 = (f32[768]{0:T(1024)S(1)}, f32[768]{0:T(1024)}, u32[]{:S(2)}) copy-start(f32[768]{0:T(1024)} %copy-done.31) | copy-start | bytes 9220
  (116 other events, 393.1 us)
Sparse Core Ops, SparseCore 0:
  10.2 68.2 all-gather.5
  80.7 39.6 all-gather.7
  122.6 78.6 all-gather.9
  203.4 78.1 all-gather.11
  493.7 66.7 reduce-scatter.6
  981.6 125.1 reduce-scatter.12
  1110.8 162.5 reduce-scatter.8
  1277.4 162.5 reduce-scatter.10
  1444.0 48.2 all-reduce.22
where the time goes:
time: 1530 us; the launch traced here: 1510 us
  waiting for transfers between devices  502 us (33%)
  matrix products  437 us (29%)
  blocking collectives  206 us (13%)
  local copies, waits for them, and re-layouts  199 us (13%)
  other arithmetic  82.2 us (5%)
  loops' own time  57.2 us (4%)
  between operations  18.3 us (1%)
    dot_general x58, matrix products, contract_cols(): lax.dot_general(left, right, (((1,), (1,)), ((), ())), preferred_element_...  184 us
    reduce_scatter x1, waiting for transfers between devices, on_device(): lax.psum_scatter(grad_down, 'shard', scatter_dimension=0, tiled=True)  164 us
    reduce_scatter x1, waiting for transfers between devices, on_device(): lax.psum_scatter(grad_up, 'shard', scatter_dimension=0, tiled=True)  164 us
    dot_general x40, matrix products, contract_rows(): lax.dot_general(left, right, (((0,), (0,)), ((), ())), preferred_element_...  111 us
    unnamed x10, waiting for transfers between devices  102 us
    all_to_all x1, blocking collectives, on_device(): lax.all_to_all(stacked[:, :, None, :], 'seq', split_axis=0, concat_axis=2...  77.3 us
    unnamed x2, blocking collectives  76.4 us
    dot_general x18, matrix products, attend(): ctx_blk = jnp.dot(probs_low, v_head, preferred_element_type=jnp.float32)  50.9 us
  transfers between devices with their start and end apart: 12, of which 6 were waited for; matrix products, arithmetic and copies ran while one was open for 43% of the time, Pallas kernels for 0%

commit v1 on v0

--- a/solution.py
+++ b/solution.py
@@ -216,8 +216,11 @@
     stacked = jnp.stack(
         [side_by_side(grad_q_heads), side_by_side(grad_k_heads), side_by_side(grad_v_heads)], axis=1
     ).astype(jnp.bfloat16)
-    grad_proj = lax.all_to_all(
-        stacked[:, :, None, :], "seq", split_axis=0, concat_axis=2, tiled=True
+    grad_proj = jnp.concatenate(
+        lax.all_to_all(
+            jnp.stack(jnp.split(stacked[:, :, None, :], lax.axis_size("seq"), axis=0)), "seq", 0, 0
+        ),
+        axis=2,
     ).reshape(tok_rows, 3 * model_width)
     grad_qkv = contract_rows(tokens, grad_proj)
     grad_q_bias = jnp.sum(grad_proj[:, :model_width], axis=0, dtype=jnp.float32)

time: 1530 us -> 1470 us (0.961)
  blocking collectives: 206 us -> 172 us
  local copies, waits for them, and re-layouts: 199 us -> 179 us
    all_to_all x1, blocking collectives: 77.3 us -> 43.7 us  [on_device(): lax.all_to_all(jnp.stack(jnp.split(stacked[:, :, None, :], lax.axis_size(...]
    unnamed x126 -> x116, local copies, waits for them, and re-layouts: 43.1 us -> 40.7 us
  transfers between devices with their start and end apart: 12 -> 12, of which waited for: 6 -> 6; matrix products, arithmetic and copies ran while one was open for 43% -> 44% of each run, Pallas kernels for 0% -> 0%
where the time goes in v1:
time: 1470 us; the launch traced here: 1460 us
  waiting for transfers between devices  500 us (34%)
  matrix products  440 us (30%)
  local copies, waits for them, and re-layouts  179 us (12%)
  blocking collectives  172 us (12%)
  other arithmetic  82.7 us (6%)
  loops' own time  57.2 us (4%)
  between operations  17.9 us (1%)
    dot_general x58, matrix products, contract_cols(): lax.dot_general(left, right, (((1,), (1,)), ((), ())), preferred_element_...  184 us
    reduce_scatter x1, waiting for transfers between devices, on_device(): lax.psum_scatter(grad_down, 'shard', scatter_dimension=0, tiled=True)  164 us
    reduce_scatter x1, waiting for transfers between devices, on_device(): lax.psum_scatter(grad_up, 'shard', scatter_dimension=0, tiled=True)  164 us
    dot_general x40, matrix products, contract_rows(): lax.dot_general(left, right, (((0,), (0,)), ((), ())), preferred_element_...  114 us
    unnamed x10, waiting for transfers between devices  100 us
    unnamed x2, blocking collectives  76.4 us
    dot_general x18, matrix products, attend(): ctx_blk = jnp.dot(probs_low, v_head, preferred_element_type=jnp.float32)  50.9 us
    dot_general x18, matrix products, block_back(): jnp.dot(grad_scores, k_head, preferred_element_type=jnp.float32)  45 us
  transfers between devices with their start and end apart: 12, of which 6 were waited for; matrix products, arithmetic and copies ran while one was open for 44% of the time, Pallas kernels for 0%

profile of v1, /device:TPU:0, one launch (start us, length us, event | category | flops | bytes accessed | tf_op | source)
XLA Modules:
  0.0 1461.4 jit_solution(13964920148770104812)
XLA Ops:
  18.1 40.2 %all-reduce.18 = (bf16[768]{0:T(1024)(128)(2,1)S(1)}, bf16[768]{0:T(1024)(128)(2,1)S(1)}, bf16[768]{0:T(1024)(128)(2,1)}, bf16[768]{0:T(1024)(128)(2,1)}, bf16[7...) all-reduce(bf16[768]{0:T(1024)(128)(2,1)S(1)} %dynamic-update-slice, ...), channel_id=1, replica_groups=mesh['seq'=4,'shard'=8] {'shard'}, use_global_device_ids=true, to_apply=%add.1 | all-reduce | flops 6144 | bytes 24576
  58.3 20.2 %all-gather.6.cloned.1.call-done = bf16[768,2304]{1,0:T(8,128)(2,1)} async-done(((bf16[96,2304]{1,0:T(8,128)(2,1)}), bf16[768,2304]{1,0:T(8,128)(2,1)}) %all-gather.6.cloned.1.call-update) | async-done | bytes 3538960 | tf_op jit(solution)/shard_map/all_gather | solution.py:71
  78.5 7.1 add_convert_fusion.1
  98.2 39.1 %all-to-all-done = bf16[768,3,4,192]{0,3,1,2:T(8,128)(2,1)S(1)} async-done(((bf16[768,3,4,192]{0,3,1,2:T(8,128)(2,1)}), bf16[768,3,4,192]{0,3,1,2:T(8,128)(2,1)S(1)}, u32[]{:S(2)}, u32[]{:S(2)}) %all-to-all-start) | async-done | bytes 3538976 | tf_op jit(solution)/shard_map/all_to_all | solution.py:84
  142.7 189.1 %while.45 = (s32[]{:T(128)}, bf16[18,512,64]{1,2,0:T(8,128)(2,1)S(1)}, f32[18,512]{1,0:T(8,128)}, s32[18]{0:T(128)S(1)}, s32[3072]{0:T(1024)S(1)}, /*index=5*/bf...) while((s32[]{:T(128)}, ...), condition=%wide.region_5.6_spmd, body=%wide.region_2.0_spmd.sunk | while | flops 416841216 | bytes 20684696 | solution.py:109
  345.3 20.4 %psum.98 = f32[]{:T(128)} all-reduce(f32[]{:T(128)} %bitcast.27), channel_id=1, replica_groups=mesh['seq'=4,'shard'=8] {'shard'}, use_global_device_ids=true, to_apply=%region_10.11 | all-reduce | flops 1 | bytes 8 | tf_op jit(solution)/shard_map/psum | solution.py:69
  367.7 25.9 %all-gather = bf16[8,1,384]{2,1,0:T(2,128)(2,1)S(1)} all-gather(bf16[1,1,384]{2,1,0:T(2,128)(2,1)S(1)} %reshape.239), channel_id=1, replica_groups=mesh['seq'=4,'shard'=8] {'shard'}, dimensions={0}, use_global_device_ids=true | all-gather | bytes 6912 | tf_op jit(solution)/shard_map/all_gather | solution.py:129
  416.6 28.8 %multiply_convert_fusion.1 = (bf16[768,3072]{1,0:T(8,128)(2,1)}, f32[768,3072]{1,0:T(8,128)}, f32[768,3072]{1,0:T(8,128)}) fusion(f32[3072]{0:T(1024)} %bitcast.169, bf16[768,3072]{1,0:T(8,128)(2,1)} %all-gather.10.cloned.1.call-done, f32[768,768]{0,1:T(8,128)S(1)} %get-tuple-element.649, f32[768]{0:T(1024)} %convert_element_type.198, ...), kind=kOutput, calls=%fused_computation.39 | convolution fusion | flops 3782541312 | bytes 30695424 | tf_op jit(solution)/shard_map/dot_general | solution.py:136
  445.4 8.0 fusion.47
  459.9 13.6 convert_reduce_fusion
  473.5 7.6 multiply_reduce_fusion.2
  493.6 11.8 all-to-all-done.2
  507.1 362.1 %while.47 = (s32[]{:T(128)}, bf16[3,3072,64]{1,2,0:T(8,128)(2,1)}, bf16[3,3072,64]{1,2,0:T(8,128)(2,1)}, bf16[3,3072,64]{1,2,0:T(8,128)(2,1)}, s32[3]{0:T(128)S(...) while((s32[]{:T(128)}, bf16[3,3072,64]{1,2,0:T(8,128)(2,1)}, ...), condition=%wide.region_19.20_spmd, body=%wide.region_15.19_spmd.sunk | while | flops 1023376896 | bytes 123100080 | solution.py:209
  516.4 109.1 %while.48 = (s32[]{:T(128)}, f32[3072,64]{0,1:T(8,128)}, f32[3072,64]{0,1:T(8,128)}, bf16[6,512,64]{1,2,0:T(8,128)(2,1)S(1)}, s32[6]{0:T(128)}, /*index=5*/s32[3...) while((s32[]{:T(128)}, f32[3072,64]{0,1:T(8,128)}, ...), condition=%wide.region_18.18_spmd.clone, body=%wide.region_16.17_spmd.clone.sunk | while | flops 1023376896 | bytes 109607288 | solution.py:204
  637.3 108.8 %while.48 = (s32[]{:T(128)}, f32[3072,64]{0,1:T(8,128)}, f32[3072,64]{0,1:T(8,128)}, bf16[6,512,64]{1,2,0:T(8,128)(2,1)S(1)}, s32[6]{0:T(128)}, /*index=5*/s32[3...) while((s32[]{:T(128)}, f32[3072,64]{0,1:T(8,128)}, ...), condition=%wide.region_18.18_spmd.clone, body=%wide.region_16.17_spmd.clone.sunk | while | flops 1023376896 | bytes 109607288 | solution.py:204
  757.9 108.8 %while.48 = (s32[]{:T(128)}, f32[3072,64]{0,1:T(8,128)}, f32[3072,64]{0,1:T(8,128)}, bf16[6,512,64]{1,2,0:T(8,128)(2,1)S(1)}, s32[6]{0:T(128)}, /*index=5*/s32[3...) while((s32[]{:T(128)}, f32[3072,64]{0,1:T(8,128)}, ...), condition=%wide.region_18.18_spmd.clone, body=%wide.region_16.17_spmd.clone.sunk | while | flops 1023376896 | bytes 109607288 | solution.py:204
  872.2 43.7 %all_to_all.53 = bf16[4,768,3,1,192]{1,4,2,3,0:T(8,128)(2,1)S(1)} all-to-all(bf16[4,768,3,1,192]{1,4,2,3,0:T(8,128)(2,1)S(1)} %pad_maximum_fusion.1), channel_id=1, replica_groups=mesh['seq'=4,'shard'=8] {'seq'}, dimensions={0} | all-to-all | bytes 7077888 | tf_op jit(solution)/shard_map/all_to_all | solution.py:220
  922.0 8.1 copy.146
  930.8 10.9 fusion.37
  941.7 10.3 fusion.49
  957.4 98.0 %reduce-scatter.13.cloned.1.call-done = f32[96,2304]{1,0:T(8,128)} async-done(((f32[768,2304]{1,0:T(8,128)}), f32[96,2304]{1,0:T(8,128)}) %reduce-scatter.13.cloned.1.call-update) | async-done | bytes 884752
  1057.6 164.3 %reduce-scatter.9.cloned.1.call-done = f32[96,3072]{1,0:T(8,128)} async-done(((f32[768,3072]{1,0:T(8,128)}), f32[96,3072]{1,0:T(8,128)}) %reduce-scatter.9.cloned.1.call-update) | async-done | bytes 1179664 | tf_op jit(solution)/shard_map/reduce_scatter | solution.py:237
  1224.1 164.5 %reduce-scatter.11.cloned.1.call-done = f32[384,768]{1,0:T(8,128)} async-done(((f32[3072,768]{1,0:T(8,128)}), f32[384,768]{1,0:T(8,128)}) %reduce-scatter.11.cloned.1.call-update) | async-done | bytes 1179664 | tf_op jit(solution)/shard_map/reduce_scatter | solution.py:239
  1400.2 36.1 %all-reduce.17 = (bf16[768]{0:T(1024)(128)(2,1)S(1)}, bf16[768]{0:T(1024)(128)(2,1)S(1)}, bf16[768]{0:T(1024)(128)(2,1)S(1)}, bf16[768]{0:T(1024)(128)(2,1)S(1)}...) all-reduce(f32[768]{0:T(1024)S(1)} %get-tuple-element.526, ...), channel_id=3, replica_groups=mesh['seq'=4,'shard'=8] {'shard'}, use_global_device_ids=true, to_apply=%region_23.24.clone | all-reduce | flops 9216 | bytes 55296
  (713 shorter events, 628.0 us)
Async XLA Ops:
  7.2 71.4 %all-gather.6.cloned.1.call-start = ((), (), s32[]{:S(2)}) async-start(), calls=%async_computation.8 | async-start | bytes 3981312 | tf_op jit(solution)/shard_map/all_gather | solution.py:71
  7.9 404.1 %all-gather.8.cloned.1.call-start = ((), (), s32[]{:S(2)}) async-start(), calls=%async_computation.9 | async-start | bytes 1327104 | tf_op jit(solution)/shard_map/all_gather | solution.py:74
  8.7 407.9 %all-gather.10.cloned.1.call-start = ((), (), s32[]{:S(2)}) async-start(), calls=%async_computation.10 | async-start | bytes 5308416 | tf_op jit(solution)/shard_map/all_gather | solution.py:128
  92.3 45.0 %all-to-all-start = ((bf16[768,3,4,192]{0,3,1,2:T(8,128)(2,1)}), bf16[768,3,4,192]{0,3,1,2:T(8,128)(2,1)S(1)}, u32[]{:S(2)}, u32[]{:S(2)}) async-start(bf16[768,3,4,192]{0,3,1,2:T(8,128)(2,1)} %copy.118), calls=%async_computation | async-start | bytes 7077888 | tf_op jit(solution)/shard_map/all_to_all | solution.py:84
  96.2 349.2 %all-gather.12.cloned.1.call-start = ((), (), s32[]{:S(2)}) async-start(), calls=%async_computation.11 | async-start | bytes 5308416 | tf_op jit(solution)/shard_map/all_gather | solution.py:130
  336.7 28.9 %copy-start.11 = (bf16[1,768,768]{2,1,0:T(8,128)(2,1)S(1)}, bf16[1,768,768]{2,1,0:T(8,128)(2,1)}, u32[]{:S(2)}) copy-start(bf16[1,768,768]{2,1,0:T(8,128)(2,1)} %param.22) | copy-start | bytes 3538948
  339.6 28.1 %copy-start.39 = (bf16[384]{0:T(512)(128)(2,1)S(1)}, bf16[384]{0:T(512)(128)(2,1)}, u32[]{:S(2)}) copy-start(bf16[384]{0:T(512)(128)(2,1)} %param.33) | copy-start | bytes 2308
  339.6 54.6 %copy-start.38 = (bf16[768]{0:T(1024)(128)(2,1)S(1)}, bf16[768]{0:T(1024)(128)(2,1)}, u32[]{:S(2)}) copy-start(bf16[768]{0:T(1024)(128)(2,1)} %get-tuple-element.601) | copy-start | bytes 4612
  339.6 54.6 %copy-start.37 = (bf16[768]{0:T(1024)(128)(2,1)S(1)}, bf16[768]{0:T(1024)(128)(2,1)}, u32[]{:S(2)}) copy-start(bf16[768]{0:T(1024)(128)(2,1)} %get-tuple-element.602) | copy-start | bytes 4612
  339.6 55.2 %copy-start.36 = (bf16[768]{0:T(1024)(128)(2,1)S(1)}, bf16[768]{0:T(1024)(128)(2,1)}, u32[]{:S(2)}) copy-start(bf16[768]{0:T(1024)(128)(2,1)} %get-tuple-element.603) | copy-start | bytes 4612
  339.6 55.8 %copy-start.10 = (bf16[1,768,768]{2,1,0:T(8,128)(2,1)S(1)}, bf16[1,768,768]{2,1,0:T(8,128)(2,1)}, u32[]{:S(2)}) copy-start(bf16[1,768,768]{2,1,0:T(8,128)(2,1)} %param.23) | copy-start | bytes 3538948
  339.6 59.9 %all-to-all-start.1 = ((bf16[4,2,73728]{2,1,0:T(2,128)(2,1)}), bf16[4,2,73728]{2,1,0:T(2,128)(2,1)}, u32[]{:S(2)}, u32[]{:S(2)}) async-start(bf16[4,2,73728]{2,1,0:T(2,128)(2,1)} %reshape.269), calls=%async_computation.1 | async-start | bytes 2359296 | tf_op jit(solution)/shard_map/all_to_all | solution.py:114
  365.7 31.4 %copy-start.35 = (bf16[768]{0:T(1024)(128)(2,1)S(1)}, bf16[768]{0:T(1024)(128)(2,1)}, u32[]{:S(2)}) copy-start(bf16[768]{0:T(1024)(128)(2,1)} %get-tuple-element.605) | copy-start | bytes 4612
  365.7 31.9 %copy-start.34 = (bf16[768]{0:T(1024)(128)(2,1)S(1)}, bf16[768]{0:T(1024)(128)(2,1)}, u32[]{:S(2)}) copy-start(bf16[768]{0:T(1024)(128)(2,1)} %get-tuple-element.606) | copy-start | bytes 4612
  414.8 66.3 %copy-start.8 = (f32[768,768]{0,1:T(8,128)}, f32[768,768]{0,1:T(8,128)S(1)}, u32[]{:S(2)}) copy-start(f32[768,768]{0,1:T(8,128)S(1)} %get-tuple-element.649) | copy-start | bytes 7077892
  414.8 66.3 %copy-start.17 = (f32[768]{0:T(1024)}, f32[768]{0:T(1024)S(1)}, u32[]{:S(2)}) copy-start(f32[768]{0:T(1024)S(1)} %broadcast_multiply_fusion.1) | copy-start | bytes 9220
  459.0 14.5 slice-start
  486.0 19.4 %all-to-all-start.2 = ((bf16[768,4,192]{0,2,1:T(8,128)(2,1)}), bf16[768,4,192]{0,2,1:T(8,128)(2,1)S(1)}, u32[]{:S(2)}, u32[]{:S(2)}) async-start(bf16[768,4,192]{0,2,1:T(8,128)(2,1)} %bitcast.166), calls=%async_computation.2 | async-start | bytes 2359296 | tf_op jit(solution)/shard_map/all_to_all | solution.py:173
  489.6 466.2 %reduce-scatter.7.cloned.1.call-start = ((), (), s32[]{:S(2)}) async-start(), calls=%async_computation.12 | async-start | bytes 2654208 | tf_op jit(solution)/shard_map/reduce_scatter | solution.py:233
  493.6 561.8 %reduce-scatter.13.cloned.1.call-start = ((), (), s32[]{:S(2)}) async-start(), calls=%async_computation.15 | async-start | bytes 7962624
  930.1 291.9 %reduce-scatter.9.cloned.1.call-start = ((), (), s32[]{:S(2)}) async-start(), calls=%async_computation.13 | async-start | bytes 10616832 | tf_op jit(solution)/shard_map/reduce_scatter | solution.py:237
  941.7 446.9 %reduce-scatter.11.cloned.1.call-start = ((), (), s32[]{:S(2)}) async-start(), calls=%async_computation.14 | async-start | bytes 10616832 | tf_op jit(solution)/shard_map/reduce_scatter | solution.py:239
  952.1 495.4 %all-reduce.23.cloned.1.call-start = ((), (), s32[]{:S(2)}) async-start(), calls=%async_computation.16 | async-start | bytes 3833856 | tf_op jit(solution)/shard_map/psum | solution.py:245
  1057.6 333.2 %copy-start.27 = (f32[768]{0:T(1024)S(1)}, f32[768]{0:T(1024)}, u32[]{:S(2)}) copy-start(f32[768]{0:T(1024)} %copy-done.26) | copy-start | bytes 9220
  (111 other events, 367.4 us)
Sparse Core Ops, SparseCore 0:
  10.2 68.2 all-gather.5
  80.7 39.6 all-gather.7
  122.6 78.6 all-gather.9
  203.3 78.0 all-gather.11
  493.7 66.6 reduce-scatter.6
  930.2 125.1 reduce-scatter.12
  1059.4 162.4 reduce-scatter.8
  1226.0 162.5 reduce-scatter.10
  1392.5 48.2 all-reduce.22
